TPU v7x, 256 devices: a whole 4x4x8 slice. The times are simulated.
256 devices in a mesh: dp: 128 (over y_hi, x, z, core), pipe: 2 (over y_lo).
Axes of the slice: x: 4, y: 4 (y_hi: 2, y_lo: 2; y = y_hi * 2 + y_lo), z: 8, core: 2. Of those that a mesh axis runs over, the one named last changes fastest.
Arguments:
- block_input: bfloat16 [2, 32768, 1536], P('pipe', 'dp'), may hold values from -100 to 100
- saved_qkv: bfloat16 [2, 32768, 4608], P('pipe', 'dp'), may hold values from -10 to 10
- cotangent: bfloat16 [2, 32768, 1536], P('pipe', 'dp'), may hold values from -6 to 6
- mod_table: float32 [2, 3, 1536], P('pipe'), may hold values from -3 to 3
- clip_condition: float32 [2, 1024, 4608], P('pipe', 'dp'), may hold values from -3 to 3
- clip_frames: int32 [2, 1024], P('pipe', 'dp'), may hold values from 0 to 8, as said below
- frame_tokens: int32 [2, 1024], P('pipe', 'dp'), may hold values from 2 to 64, as said below
- tile_layout: int32 [2, 256, 2], P('pipe', 'dp'), may hold values from 0 to 1, as said below
- frozen_qkv: bfloat16 [2, 1536, 4608], P('pipe', 'dp'), may hold values from -0.15625 to 0.15625
- frozen_out: bfloat16 [2, 1536, 1536], P('pipe', 'dp'), may hold values from -0.15625 to 0.15625
- adapters: bfloat16 [2, 9216, 128], P('pipe'), may hold values from -0.15625 to 0.15625
Outputs:
- upstream: bfloat16 [2, 32768, 1536], P('pipe', 'dp')
- d_table: float32 [2, 3, 1536], P('pipe')
- d_adapters: float32 [2, 9216, 128], P('pipe', 'dp')
Inputs may be any that keep to these rules, and one draw needn't show every extreme that they name: `clip_frames`: clips are packed in slot order; a slot with 0 frames holds no clip and so does every later slot of that device; the clips of one device hold at most 256 tokens. `frame_tokens`: even. `tile_layout`: every diagonal tile is live.
All inputs are finite; a program needn't handle non-finite values.
Results may differ from a plain program's by a relative error of at most 0.0065.
Values may be sent and summed in bfloat16 or wider, within the bound.
A program may use at most 128 MiB of HBM per device.

v0:
```python
import jax
import jax.numpy as jnp
from jax import lax
from jax.sharding import PartitionSpec as P

HEAD = 128
TILE = 128
EPSILON = 1e-06
HIGH = lax.Precision.HIGHEST


def passed_along(block, axis, distance):
    devices = range(lax.axis_size(axis))
    route = [((i - distance) % len(devices), i) for i in devices]
    return lax.ppermute(block, axis, route)


def contract_last(left, right):
    return lax.dot_general(
        left, right, (((1,), (1,)), ((), ())), preferred_element_type=jnp.float32
    )


def contract_first(left, right):
    return lax.dot_general(
        left, right, (((0,), (0,)), ((), ())), preferred_element_type=jnp.float32
    )


def on_device(
    block_input,
    saved_qkv,
    cotangent,
    mod_table,
    clip_condition,
    clip_frames,
    frame_tokens,
    tile_layout,
    frozen_qkv,
    frozen_out,
    adapters,
):
    tokens_here = block_input[0]
    rows, width = tokens_here.shape
    saved = saved_qkv[0]
    inner = saved.shape[1] // 3
    heads = inner // HEAD
    slots = clip_frames.shape[1]
    tiles = tile_layout.shape[1]
    adapter_rows = adapters[0]
    down_qkv = adapter_rows[:width]
    up_qkv = adapter_rows[width : width + 3 * inner]
    down_out = adapter_rows[width + 3 * inner : width + 4 * inner]
    up_out = adapter_rows[width + 4 * inner :]
    clip_ends = jnp.cumsum(clip_frames[0] * frame_tokens[0])
    position = jnp.arange(rows, dtype=jnp.int32)
    clip_of = jnp.sum((position[:, None] >= clip_ends[None, :]).astype(jnp.int32), axis=1)
    onehot_clip = (clip_of[:, None] == jnp.arange(slots, dtype=jnp.int32)[None, :]).astype(
        jnp.float32
    )
    modulation = mod_table[0].reshape(1, 3 * width) + jnp.dot(
        onehot_clip, clip_condition[0], precision=HIGH
    )
    shift_rows = modulation[:, :width]
    scale_rows = modulation[:, width : 2 * width]
    gate_rows = modulation[:, 2 * width :]
    inputs_f = tokens_here.astype(jnp.float32)
    centered = inputs_f - jnp.mean(inputs_f, axis=1, keepdims=True)
    inverse = lax.rsqrt(jnp.mean(centered * centered, axis=1, keepdims=True) + EPSILON)
    normed = centered * inverse
    modded = (normed * (1.0 + scale_rows) + shift_rows).astype(jnp.bfloat16)
    tile_onehot = (
        (position // TILE)[:, None] == jnp.arange(tiles, dtype=jnp.int32)[None, :]
    ).astype(jnp.float32)
    live_rows = jnp.dot(tile_onehot, tile_layout[0].astype(jnp.float32), precision=HIGH)
    live_pairs = jnp.dot(live_rows, tile_onehot.T, precision=HIGH) > 0.5
    allowed = live_pairs & (clip_of[:, None] == clip_of[None, :])
    queries = saved[:, :inner].reshape(rows, heads, HEAD)
    key_rows = saved[:, inner : 2 * inner].reshape(rows, heads, HEAD)
    value_rows = saved[:, 2 * inner :].reshape(rows, heads, HEAD)
    factor = HEAD ** (-0.5)
    scores = (
        jnp.einsum("qhd,khd->hqk", queries, key_rows, preferred_element_type=jnp.float32) * factor
    )
    scores = jnp.where(allowed[None], scores, -jnp.inf)
    probs = jax.nn.softmax(scores, axis=2)
    probs_b = probs.astype(jnp.bfloat16)
    attention = (
        jnp.einsum("hqk,khd->qhd", probs_b, value_rows, preferred_element_type=jnp.float32)
        .reshape(rows, inner)
        .astype(jnp.bfloat16)
    )
    out_whole = lax.all_gather(frozen_out[0], "dp", axis=0, tiled=True)
    low_out = jnp.dot(attention, down_out, preferred_element_type=jnp.float32).astype(jnp.bfloat16)
    branch = jnp.dot(attention, out_whole, preferred_element_type=jnp.float32) + contract_last(
        low_out, up_out
    )
    cotangent_f = cotangent[0].astype(jnp.float32)
    gated = (gate_rows * cotangent_f).astype(jnp.bfloat16)
    low_grad_out = jnp.dot(gated, up_out, preferred_element_type=jnp.float32).astype(jnp.bfloat16)
    grad_attention = (
        contract_last(gated, out_whole) + contract_last(low_grad_out, down_out)
    ).astype(jnp.bfloat16)
    grad_heads = grad_attention.reshape(rows, heads, HEAD)
    grad_probs = jnp.einsum(
        "qhd,khd->hqk", grad_heads, value_rows, preferred_element_type=jnp.float32
    )
    delta = jnp.sum(probs * grad_probs, axis=2, keepdims=True)
    grad_scores = (probs * (grad_probs - delta) * factor).astype(jnp.bfloat16)
    grad_query = jnp.einsum(
        "hqk,khd->qhd", grad_scores, key_rows, preferred_element_type=jnp.float32
    ).reshape(rows, inner)
    grad_key = jnp.einsum(
        "hqk,qhd->khd", grad_scores, queries, preferred_element_type=jnp.float32
    ).reshape(rows, inner)
    grad_value = jnp.einsum(
        "hqk,qhd->khd", probs_b, grad_heads, preferred_element_type=jnp.float32
    ).reshape(rows, inner)
    grad_qkv = jnp.concatenate([grad_query, grad_key, grad_value], axis=1).astype(jnp.bfloat16)
    low_in = jnp.dot(modded, down_qkv, preferred_element_type=jnp.float32).astype(jnp.bfloat16)
    low_grad_in = jnp.dot(grad_qkv, up_qkv, preferred_element_type=jnp.float32).astype(jnp.bfloat16)
    frozen_part = contract_last(grad_qkv, lax.all_gather(frozen_qkv[0], "dp", axis=0, tiled=True))
    grad_modded = frozen_part + contract_last(low_grad_in, down_qkv)
    grad_normed = grad_modded * (1.0 + scale_rows)
    grad_input = cotangent_f + inverse * (
        grad_normed
        - jnp.mean(grad_normed, axis=1, keepdims=True)
        - normed * jnp.mean(grad_normed * normed, axis=1, keepdims=True)
    )
    grad_input = grad_input.astype(jnp.bfloat16)
    table_part = jnp.stack(
        [
            jnp.sum(grad_modded, axis=0),
            jnp.sum(grad_modded * normed, axis=0),
            jnp.sum(cotangent_f * branch, axis=0),
        ]
    )
    adapter_part = jnp.concatenate(
        [
            contract_first(modded, low_grad_in),
            contract_first(grad_qkv, low_in),
            contract_first(attention, low_grad_out),
            contract_first(gated, low_out),
        ],
        axis=0,
    )
    replicas = lax.axis_size("dp")
    table_sum = lax.psum(table_part, "dp")
    adapter_sum = lax.psum_scatter(adapter_part, "dp", scatter_dimension=0, tiled=True)
    passed_back = passed_along(grad_input, "pipe", -1)
    return (passed_back[None], (table_sum / replicas)[None], (adapter_sum / replicas)[None])


def solution(mesh):
    placed = (
        P("pipe", "dp", None),
        P("pipe", "dp", None),
        P("pipe", "dp", None),
        P("pipe", None, None),
        P("pipe", "dp", None),
        P("pipe", "dp"),
        P("pipe", "dp"),
        P("pipe", "dp", None),
        P("pipe", "dp", None),
        P("pipe", "dp", None),
        P("pipe", None, None),
    )
    return jax.shard_map(
        on_device,
        mesh=mesh,
        in_specs=placed,
        out_specs=(P("pipe", "dp", None), P("pipe", None, None), P("pipe", "dp", None)),
        check_vma=False,
    )
```

profile of v0, /device:TPU:24, one launch (start us, length us, event | category | flops | bytes accessed | tf_op | source)
XLA Modules:
  0.0 1030.8 jit_solution(3431634579124080414)
XLA Ops:
  7.2 1.5 copy.65
  8.8 1.8 copy.72
  12.4 0.9 fusion.79
  13.9 2.9 copy.62
  17.4 1.5 fusion.92
  18.9 4.2 fusion.93
  23.1 2.3 convolution_convert_fusion
  25.4 1.7 convolution_convert_fusion.3
  27.1 2.0 convolution_add_fusion
  29.5 1.7 convolution_convert_fusion.4
  31.6 1.3 fusion.97
  33.0 111.5 %all-gather.5.cloned.1.call-done = bf16[1,1536,1536]{2,0,1:T(2,128)(2,1)} async-done(((bf16[1,12,1536]{2,0,1:T(2,128)(2,1)}), bf16[1,1536,1536]{2,0,1:T(2,128)(2,1)}) %all-gather.5.cloned.1.call-update) | async-done | bytes 4718608 | tf_op jit(solution)/shard_map/all_gather | solution.py:93
  144.5 5.4 fusion.7
  149.8 2.2 fusion.11
  152.1 2.3 copy.66
  154.4 3.4 fusion.94
  157.8 7.1 fusion.44
  164.9 6.9 fusion.47
  171.8 2.7 convolution_convert_fusion.1
  174.5 0.9 copy-done.16
  176.2 153.9 %all-gather.7.cloned.1.call-done = bf16[1,1536,4608]{2,0,1:T(2,128)(2,1)} async-done(((bf16[1,12,4608]{2,0,1:T(2,128)(2,1)}), bf16[1,1536,4608]{2,0,1:T(2,128)(2,1)}) %all-gather.7.cloned.1.call-update) | async-done | bytes 14155792 | tf_op jit(solution)/shard_map/all_gather | solution.py:122
  330.1 14.6 %fusion.2 = f32[256,1536]{1,0:T(8,128)S(1)} fusion(bf16[1,1536,4608]{2,0,1:T(2,128)(2,1)} %all-gather.7.cloned.1.call-done, bf16[256,1536]{0,1:T(8,128)(2,1)} %bitcast.145, bf16[256,1536]{0,1:T(8,128)(2,1)} %bitcast.141, bf16[256,1536]{0,1:T(8,128)(2,1)S(1)} %bitcast.140), kind=kOutput, calls=%fused_computation.2 | convolution fusion | flops 3630956544 | bytes 18087936 | tf_op jit(solution)/shard_map/dot_general | solution.py:19
  344.8 2.4 fusion.91
  347.2 3.6 fusion.35
  350.8 4.3 fusion.58
  355.5 6.9 pad_maximum_fusion
  362.4 1.1 copy-done.11
  363.6 5.2 fusion.5
  368.8 1.4 fusion.51
  370.3 651.1 %psum.7 = f32[3,1536]{1,0:T(4,128)S(1)} all-reduce(f32[3,1536]{1,0:T(4,128)S(1)} %pad_maximum_fusion.2), channel_id=1, replica_groups=mesh['dp'=128,'pipe'=2] {'dp'}, use_global_device_ids=true, to_apply=%region_12.13 | all-reduce | flops 4608 | bytes 36864 | tf_op jit(solution)/shard_map/psum | solution.py:148
  1022.0 1.4 multiply_bitcast_fusion
  1023.4 0.9 copy.97
  (64 shorter events, 5.9 us)
Async XLA Ops:
  7.2 20.0 %copy-start = (f32[1,8,4608]{2,1,0:T(8,128)S(1)}, f32[1,8,4608]{2,1,0:T(8,128)}, u32[]{:S(2)}) copy-start(f32[1,8,4608]{2,1,0:T(8,128)} %param.15) | copy-start | bytes 442372
  7.2 137.3 %all-gather.5.cloned.1.call-start = ((), (), s32[]{:S(2)}) async-start(), calls=%async_computation.1 | async-start | bytes 9510912 | tf_op jit(solution)/shard_map/all_gather | solution.py:93
  8.8 321.4 %all-gather.7.cloned.1.call-start = ((), (), s32[]{:S(2)}) async-start(), calls=%async_computation.2 | async-start | bytes 28532736 | tf_op jit(solution)/shard_map/all_gather | solution.py:122
  10.6 1011.4 %reduce-scatter.4.cloned.1.call-start = ((), (), s32[]{:S(2)}) async-start(), calls=%async_computation.3 | async-start | bytes 4755456
  13.9 2.9 copy-start.3
  18.9 4.2 copy-start.5
  25.4 5.7 copy-start.10
  27.1 2.1 copy-start.4
  29.2 2.3 copy-start.2
  29.5 2.2 copy-start.8
  164.9 6.9 copy-start.7
  171.8 3.6 copy-start.12
  171.8 3.6 copy-start.13
  171.8 3.6 copy-start.15
  174.5 0.9 copy-start.16
  175.4 154.7 %copy-start.14 = (bf16[12,256,128]{1,2,0:T(8,128)(2,1)S(1)}, bf16[12,256,128]{1,2,0:T(8,128)(2,1)}, u32[]{:S(2)}) copy-start(bf16[12,256,128]{1,2,0:T(8,128)(2,1)} %fusion.44) | copy-start | bytes 2359300
  350.8 4.7 copy-start.6
  362.4 1.1 copy-start.11
  363.6 5.2 copy-start.9
  363.6 660.8 %copy-start.1 = (f32[1,8,4608]{2,1,0:T(8,128)S(1)}, f32[1,8,4608]{2,1,0:T(8,128)}, u32[]{:S(2)}) copy-start(f32[1,8,4608]{2,1,0:T(8,128)} %param.15) | copy-start | bytes 442372
  368.7 653.3 %collective-permute-start = (bf16[256,1536]{1,0:T(8,128)(2,1)S(1)}, bf16[256,1536]{1,0:T(8,128)(2,1)S(1)}, u32[]{:S(2)}, u32[]{:S(2)}) collective-permute-start(bf16[256,1536]{1,0:T(8,128)(2,1)S(1)} %copy-done.9), channel_id=1, source_target_pairs={{1,0},{0,1},{3,2},{2,3},{5,4},{4,5},{7,6},{6,7},{9,8},{8,9},{11,10... | collective-permute-start | bytes 2359304 | tf_op jit(solution)/shard_map/ppermute | solution.py:15
Sparse Core Ops, SparseCore 0:
  11.9 132.5 all-gather.4
  148.3 181.7 all-gather.6
  362.6 268.5 reduce-scatter.3
where the time goes:
time: 1030 us
  blocking collectives  651 us (63%)
  waiting for transfers between devices  265 us (26%)
  matrix products  71.8 us (7%)
  other arithmetic  14.4 us (1%)
  between operations  14 us (1%)
  local copies, waits for them, and re-layouts  13.9 us (1%)
    psum x1, blocking collectives, on_device(): table_sum = lax.psum(table_part, 'dp')  651 us
    all_gather x1, waiting for transfers between devices, on_device(): lax.all_gather(frozen_qkv[0], 'dp', axis=0, tiled=True)  154 us
    all_gather x1, waiting for transfers between devices, on_device(): out_whole = lax.all_gather(frozen_out[0], 'dp', axis=0, tiled=True)  111 us
    dot_general x5, matrix products, contract_last(): lax.dot_general(left, right, (((1,), (1,)), ((), ())), preferred_element_...  26 us
  transfers between devices with their start and end apart: 4, of which 2 were waited for; matrix products, arithmetic and copies ran while one was open for 6% of the time, Pallas kernels for 0%

commit v1 on v0

--- a/solution.py
+++ b/solution.py
@@ -145,7 +145,8 @@
         axis=0,
     )
     replicas = lax.axis_size("dp")
-    table_sum = lax.psum(table_part, "dp")
+    blocks = lax.all_gather(table_part, "dp", axis=0, tiled=False)
+    table_sum = blocks.sum(axis=0)
     adapter_sum = lax.psum_scatter(adapter_part, "dp", scatter_dimension=0, tiled=True)
     passed_back = passed_along(grad_input, "pipe", -1)
     return (passed_back[None], (table_sum / replicas)[None], (adapter_sum / replicas)[None])

time: 1030 us -> 746 us (0.72)
  blocking collectives: 651 us -> 0 us
  waiting for transfers between devices: 265 us -> 626 us
    psum x1 -> x0, blocking collectives: 651 us -> none  [on_device(): table_sum = lax.psum(table_part, 'dp')]
    unnamed x4 -> x5, waiting for transfers between devices: 0.05 us -> 271 us
    all_gather x0 -> x1, waiting for transfers between devices: none -> 71.3 us  [on_device(): blocks = lax.all_gather(table_part, 'dp', axis=0, tiled=False)]
    ppermute x1, waiting for transfers between devices: 0.01 us -> 19.7 us  [passed_along(): return lax.ppermute(block, axis, route)]
  transfers between devices with their start and end apart: 4 -> 5, of which waited for: 2 -> 5; matrix products, arithmetic and copies ran while one was open for 6% -> 10% of each run, Pallas kernels for 0% -> 0%
where the time goes in v1:
time: 746 us; the launch traced here: 744 us
  waiting for transfers between devices  626 us (84%)
  matrix products  70.2 us (9%)
  other arithmetic  17.4 us (2%)
  local copies, waits for them, and re-layouts  16.7 us (2%)
  between operations  14 us (2%)
    unnamed x5, waiting for transfers between devices  271 us
    all_gather x1, waiting for transfers between devices, on_device(): lax.all_gather(frozen_qkv[0], 'dp', axis=0, tiled=True)  153 us
    all_gather x1, waiting for transfers between devices, on_device(): out_whole = lax.all_gather(frozen_out[0], 'dp', axis=0, tiled=True)  111 us
    all_gather x1, waiting for transfers between devices, on_device(): blocks = lax.all_gather(table_part, 'dp', axis=0, tiled=False)  71.3 us
    dot_general x5, matrix products, contract_last(): lax.dot_general(left, right, (((1,), (1,)), ((), ())), preferred_element_...  22 us
    ppermute x1, waiting for transfers between devices, passed_along(): return lax.ppermute(block, axis, route)  19.7 us
  transfers between devices with their start and end apart: 5, of which 5 were waited for; matrix products, arithmetic and copies ran while one was open for 10% of the time, Pallas kernels for 0%

profile of v1, /device:TPU:24, one launch (start us, length us, event | category | flops | bytes accessed | tf_op | source)
XLA Modules:
  0.0 744.2 jit_solution(3601790440997639089)
XLA Ops:
  7.2 1.5 copy.65
  8.8 1.8 copy.72
  13.9 2.9 copy.62
  17.4 1.5 fusion.92
  18.9 4.2 fusion.93
  23.1 2.3 convolution_convert_fusion
  26.3 1.4 convolution_convert_fusion.3
  27.7 2.0 convolution_add_fusion
  29.8 2.1 copy-done.2
  32.1 1.6 convolution_convert_fusion.4
  33.8 110.7 %all-gather.8.cloned.1.call-done = bf16[1,1536,1536]{2,0,1:T(2,128)(2,1)} async-done(((bf16[1,12,1536]{2,0,1:T(2,128)(2,1)}), bf16[1,1536,1536]{2,0,1:T(2,128)(2,1)}) %all-gather.8.cloned.1.call-update) | async-done | bytes 4718608 | tf_op jit(solution)/shard_map/all_gather | solution.py:93
  144.5 5.5 fusion.5
  149.9 1.5 fusion.51
  151.5 1.4 fusion.7
  152.9 2.2 fusion.11
  155.2 1.4 copy.66
  156.6 2.4 fusion.94
  158.9 7.1 fusion.44
  166.0 6.8 fusion.47
  172.8 2.7 convolution_convert_fusion.1
  177.4 152.7 %all-gather.10.cloned.1.call-done = bf16[1,1536,4608]{2,0,1:T(2,128)(2,1)} async-done(((bf16[1,12,4608]{2,0,1:T(2,128)(2,1)}), bf16[1,1536,4608]{2,0,1:T(2,128)(2,1)}) %all-gather.10.cloned.1.call-update) | async-done | bytes 14155792 | tf_op jit(solution)/shard_map/all_gather | solution.py:122
  330.1 14.4 %fusion.2 = f32[256,1536]{1,0:T(8,128)S(1)} fusion(bf16[1,1536,4608]{2,0,1:T(2,128)(2,1)} %all-gather.10.cloned.1.call-done, bf16[256,1536]{0,1:T(8,128)(2,1)} %bitcast.147, bf16[256,1536]{0,1:T(8,128)(2,1)S(1)} %bitcast.145, bf16[256,1536]{0,1:T(8,128)(2,1)S(1)} %bitcast.142), kind=kOutput, calls=%fused_computation.2 | convolution fusion | flops 3630956544 | bytes 18087936 | tf_op jit(solution)/shard_map/dot_general | solution.py:19
  344.5 2.4 fusion.91
  347.7 2.4 fusion.96
  350.1 2.5 fusion.97
  352.6 3.6 fusion.35
  357.5 4.6 fusion.58
  362.1 6.9 pad_maximum_fusion
  370.1 19.7 %collective-permute-done = bf16[256,1536]{1,0:T(8,128)(2,1)S(1)} collective-permute-done((bf16[256,1536]{1,0:T(8,128)(2,1)S(1)}, bf16[256,1536]{1,0:T(8,128)(2,1)S(1)}, u32[]{:S(2)}, u32[]{:S(2)}) %collective-permute-start) | collective-permute-done | bytes 786464 | tf_op jit(solution)/shard_map/ppermute | solution.py:15
  389.8 71.3 %all-gather.12.cloned.1.call-done = f32[128,3,1536]{2,1,0:T(4,128)} async-done(((f32[1,3,1536]{2,1,0:T(4,128)}), f32[128,3,1536]{2,1,0:T(4,128)}) %all-gather.12.cloned.1.call-update) | async-done | bytes 2359312 | tf_op jit(solution)/shard_map/all_gather | solution.py:148
  461.1 2.4 reduce_sum.109
  464.1 271.3 %reduce-scatter.4.cloned.1.call-done = f32[72,128]{1,0:T(8,128)} async-done(((f32[9216,128]{1,0:T(8,128)}), f32[72,128]{1,0:T(8,128)}) %reduce-scatter.4.cloned.1.call-update) | async-done | bytes 36880
  (71 shorter events, 13.0 us)
Async XLA Ops:
  7.2 20.5 %copy-start = (f32[1,8,4608]{2,1,0:T(8,128)S(1)}, f32[1,8,4608]{2,1,0:T(8,128)}, u32[]{:S(2)}) copy-start(f32[1,8,4608]{2,1,0:T(8,128)} %param.15) | copy-start | bytes 442372
  7.2 137.3 %all-gather.8.cloned.1.call-start = ((), (), s32[]{:S(2)}) async-start(), calls=%async_computation.1 | async-start | bytes 9510912 | tf_op jit(solution)/shard_map/all_gather | solution.py:93
  8.8 321.4 %all-gather.10.cloned.1.call-start = ((), (), s32[]{:S(2)}) async-start(), calls=%async_computation.2 | async-start | bytes 28532736 | tf_op jit(solution)/shard_map/all_gather | solution.py:122
  10.6 450.5 %all-gather.12.cloned.1.call-start = ((), (), s32[]{:S(2)}) async-start(), calls=%async_computation.3 | async-start | bytes 3170304 | tf_op jit(solution)/shard_map/all_gather | solution.py:148
  13.9 2.9 copy-start.3
  18.9 4.2 copy-start.5
  25.4 0.9 copy-start.12
  27.7 4.2 copy-start.4
  29.7 2.2 copy-start.2
  32.1 119.3 %copy-start.9 = (bf16[256,1536]{1,0:T(8,128)(2,1)}, bf16[256,1536]{1,0:T(8,128)(2,1)S(1)}, u32[]{:S(2)}) copy-start(bf16[256,1536]{1,0:T(8,128)(2,1)S(1)} %fusion.37) | copy-start | bytes 2359300
  144.5 7.0 copy-start.14
  158.9 7.1 copy-start.10
  172.8 3.6 copy-start.13
  172.8 3.6 copy-start.15
  172.8 3.6 copy-start.16
  175.5 0.9 copy-start.18
  176.4 153.7 %copy-start.17 = (bf16[12,256,128]{1,2,0:T(8,128)(2,1)S(1)}, bf16[12,256,128]{1,2,0:T(8,128)(2,1)}, u32[]{:S(2)}) copy-start(bf16[12,256,128]{1,2,0:T(8,128)(2,1)} %fusion.47) | copy-start | bytes 2359300
  347.6 387.7 %reduce-scatter.4.cloned.1.call-start = ((), (), s32[]{:S(2)}) async-start(), calls=%async_computation.4 | async-start | bytes 4755456
  356.1 0.9 copy-start.8
  357.4 4.7 copy-start.6
  357.4 4.7 copy-start.7
  369.0 1.1 copy-start.11
  370.1 19.7 %collective-permute-start = (bf16[256,1536]{1,0:T(8,128)(2,1)S(1)}, bf16[256,1536]{1,0:T(8,128)(2,1)S(1)}, u32[]{:S(2)}, u32[]{:S(2)}) collective-permute-start(bf16[256,1536]{1,0:T(8,128)(2,1)S(1)} %copy-done.11), channel_id=1, source_target_pairs={{1,0},{0,1},{3,2},{2,3},{5,4},{4,5},{7,6},{6,7},{9,8},{8,9},{11,10... | collective-permute-start | bytes 2359304 | tf_op jit(solution)/shard_map/ppermute | solution.py:15
  389.8 347.8 %copy-start.1 = (f32[1,8,4608]{2,1,0:T(8,128)S(1)}, f32[1,8,4608]{2,1,0:T(8,128)}, u32[]{:S(2)}) copy-start(f32[1,8,4608]{2,1,0:T(8,128)} %param.15) | copy-start | bytes 442372
Sparse Core Ops, SparseCore 0:
  11.9 132.5 all-gather.7
  148.3 181.7 all-gather.9
  347.8 113.2 all-gather.11
  466.9 268.4 reduce-scatter.3
